TPU v7x, 32 devices: a whole 2x2x4 slice. The times are simulated.
32 devices in a mesh: ep: 16 (over z, x, core), hs: 2 (over y).
Axes of the slice: x: 2, y: 2, z: 4, core: 2. Of those that a mesh axis runs over, the one named last changes fastest.
Arguments:
- tokens: bfloat16 [8192, 1024], P(('ep', 'hs')), may hold values from -6 to 6
- segment_ids: int32 [32, 256], P(('ep', 'hs')), may hold values from 0 to 3, never falling along the last dimension, each value on 1 to 128 neighbouring positions
- live_mask: int32 [32, 256], P(('ep', 'hs')), may hold values 0 or 1
- routes: int32 [8192, 8], P(('ep', 'hs')), may hold values from 0 to 15, all different within a row; in each aligned block of 256 rows (0 to 255, 256 to 511, ...) at most 256 rows name the same one
- attn_gain: float32 [1024], replicated, may hold values from 0.25 to 1.75
- w_query: bfloat16 [1024, 1024], replicated, may hold values from -0.1875 to 0.1875
- key_weight: bfloat16 [1024, 512], replicated, may hold values from -0.1875 to 0.1875
- value_weight: bfloat16 [1024, 512], replicated, may hold values from -0.1875 to 0.1875
- w_out: bfloat16 [1024, 1024], replicated, may hold values from -1 to 1
- moe_gain: float32 [1024], replicated, may hold values from 0.25 to 1.75
- router: bfloat16 [1024, 16], replicated, may hold values from -0.09375 to 0.09375
- w_gate: bfloat16 [16, 1024, 512], P('ep', None, 'hs'), may hold values from -0.1875 to 0.1875
- w_up: bfloat16 [16, 1024, 512], P('ep', None, 'hs'), may hold values from -0.1875 to 0.1875
- w_down: bfloat16 [16, 512, 1024], P('ep', 'hs'), may hold values from -0.75 to 0.75
- cotangent: bfloat16 [8192, 1024], P(('ep', 'hs')), may hold values from -6 to 6
Outputs:
- output: bfloat16 [8192, 1024], P(('ep', 'hs'))
- input_grad: float32 [8192, 1024], P(('ep', 'hs'))
- attn_gain_grad: float32 [1024], replicated
- query_grad: float32 [1024, 1024], replicated
- key_grad: float32 [1024, 512], replicated
- value_grad: float32 [1024, 512], replicated
- out_grad: float32 [1024, 1024], replicated
- moe_gain_grad: float32 [1024], replicated
- router_grad: float32 [1024, 16], replicated
- gate_grad: float32 [16, 1024, 512], P('ep', None, 'hs')
- up_grad: float32 [16, 1024, 512], P('ep', None, 'hs')
- down_grad: float32 [16, 512, 1024], P('ep', 'hs')
- expert_counts: int32 [16], replicated
Inputs may be any that keep to these rules, and one draw needn't show every extreme that they name: `segment_ids`: document numbers never fall along a row; a document has at most 128 tokens, and one has exactly that many. `routes`: each token names 8 different experts. The 256 tokens of one row name one expert at most 256 times, a bound that some block reaches.
All inputs are finite; a program needn't handle non-finite values. No bound on the sum of `live_mask` on one device may be relied on, other than what follows from the above.
Results may differ from a plain program's by a relative error of at most 0.013.
The roundings to bfloat16 on the way count: a program that leaves them out, or rounds other values in their place, can miss the bound.
Values may be sent and summed in bfloat16 or wider, within the bound.
A program may use at most 384 MiB of HBM per device.

v0:
```python
import jax
import jax.numpy as jnp
from jax import lax
from jax.sharding import PartitionSpec as P

QUERY_HEADS = 16
KEY_VALUE_HEADS = 8
HEAD_SIZE = 64
TOP = 8
EPSILON = 1e-05


def rms_forward(value_rows, norm_gain):
    inverse = lax.rsqrt(jnp.mean(value_rows * value_rows, axis=-1, keepdims=True) + EPSILON)
    return (value_rows * inverse * norm_gain, inverse)


def rms_backward(value_rows, inverse, norm_gain, upstream):
    scaled = upstream * norm_gain
    gain_grad = jnp.sum(upstream * value_rows * inverse, axis=0)
    input_grad = inverse * (
        scaled
        - value_rows * inverse * inverse * jnp.mean(scaled * value_rows, axis=-1, keepdims=True)
    )
    return (input_grad, gain_grad)


def positions_of(segment):
    before = (segment[None, :] < segment[:, None]).astype(jnp.int32)
    return jnp.arange(segment.shape[-1], dtype=jnp.int32) - jnp.sum(before, axis=1)


def rotary_tables(positions, head_dim):
    half_dim = head_dim // 2
    frequency = 10000.0 ** (-(jnp.arange(half_dim, dtype=jnp.float32) * 2.0) / head_dim)
    angles = positions.astype(jnp.float32)[:, None] * frequency[None, :]
    return (jnp.cos(angles)[:, None, :], jnp.sin(angles)[:, None, :])


def rotary(heads, cosine_table, sine_table):
    half_dim = heads.shape[-1] // 2
    first_half = heads[..., :half_dim]
    second_half = heads[..., half_dim:]
    return jnp.concatenate(
        [
            first_half * cosine_table - second_half * sine_table,
            second_half * cosine_table + first_half * sine_table,
        ],
        axis=-1,
    )


def rotary_backward(grads, cosine_table, sine_table):
    half_dim = grads.shape[-1] // 2
    first_half = grads[..., :half_dim]
    second_half = grads[..., half_dim:]
    return jnp.concatenate(
        [
            first_half * cosine_table + second_half * sine_table,
            second_half * cosine_table - first_half * sine_table,
        ],
        axis=-1,
    )


def to_bf16(value):
    return lax.reduce_precision(value, 8, 7)


def expert_pass(rows, upstream, gates, gate_w, up_w, down_w):
    groups, model_dim, width = gate_w.shape
    gate_all = jnp.concatenate([gate_w[j] for j in range(groups)], axis=1)
    up_all = jnp.concatenate([up_w[j] for j in range(groups)], axis=1)
    down_all = down_w.reshape(groups * width, model_dim)
    gate_pre = jnp.dot(rows, gate_all, preferred_element_type=jnp.float32)
    up_pre = jnp.dot(rows, up_all, preferred_element_type=jnp.float32)
    sigmoid_part = jax.nn.sigmoid(gate_pre)
    activated = gate_pre * sigmoid_part
    hidden = (activated * up_pre).astype(jnp.bfloat16)
    total = jnp.zeros(rows.shape, jnp.float32)
    for j in range(groups):
        total = total + to_bf16(
            jnp.dot(
                hidden[:, j * width : (j + 1) * width],
                down_w[j],
                preferred_element_type=jnp.float32,
            )
        )
    total = to_bf16(total)
    upstream_f = upstream.astype(jnp.float32)
    gate_upstream = jnp.sum(upstream_f * total, axis=-1)
    weighted = (gates[:, None] * total).astype(jnp.bfloat16)
    upstream_e = (gates[:, None] * upstream_f).astype(jnp.bfloat16)
    hidden_grad = jnp.einsum("td,fd->tf", upstream_e, down_all, preferred_element_type=jnp.float32)
    up_pre_grad = (hidden_grad * activated).astype(jnp.bfloat16)
    gate_pre_grad = (
        hidden_grad * up_pre * sigmoid_part * (1.0 + gate_pre * (1.0 - sigmoid_part))
    ).astype(jnp.bfloat16)
    down_grad = jnp.einsum("tf,td->fd", hidden, upstream_e, preferred_element_type=jnp.float32)
    gate_grad = jnp.einsum("td,tf->df", rows, gate_pre_grad, preferred_element_type=jnp.float32)
    up_grad = jnp.einsum("td,tf->df", rows, up_pre_grad, preferred_element_type=jnp.float32)
    back = jnp.zeros(rows.shape, jnp.float32)
    for j in range(groups):
        cut = slice(j * width, (j + 1) * width)
        back = back + to_bf16(
            jnp.einsum(
                "tf,df->td", gate_pre_grad[:, cut], gate_w[j], preferred_element_type=jnp.float32
            )
            + jnp.einsum(
                "tf,df->td", up_pre_grad[:, cut], up_w[j], preferred_element_type=jnp.float32
            )
        )
    return (weighted, back.astype(jnp.bfloat16), gate_upstream, gate_grad, up_grad, down_grad)


def local(
    tokens,
    segment_ids,
    live_mask,
    routes,
    attn_gain,
    w_query,
    key_weight,
    value_weight,
    w_out,
    moe_gain,
    router,
    w_gate,
    w_up,
    w_down,
    cotangent,
):
    sequence_length = tokens.shape[0]
    model_dim = tokens.shape[1]
    experts_all = router.shape[1]
    query_per_key_head = QUERY_HEADS // KEY_VALUE_HEADS
    score_scale = HEAD_SIZE ** (-0.5)
    upstream_all = lax.all_gather(cotangent, "ep", axis=0, tiled=True)
    gate_all = lax.all_gather(w_gate, "hs", axis=0, tiled=True)
    up_all = lax.all_gather(w_up, "hs", axis=0, tiled=True)
    down_all = lax.all_gather(w_down, "hs", axis=0, tiled=True)
    segment = segment_ids[0]
    live_row = live_mask[0]
    inputs = tokens.astype(jnp.float32)
    normed_rows, inverse_one = rms_forward(inputs, attn_gain)
    normed_rows_back = normed_rows.astype(jnp.bfloat16)
    query_pre = jnp.dot(normed_rows_back, w_query, preferred_element_type=jnp.float32).reshape(
        sequence_length, QUERY_HEADS, HEAD_SIZE
    )
    key_before_rotary = jnp.dot(
        normed_rows_back, key_weight, preferred_element_type=jnp.float32
    ).reshape(sequence_length, KEY_VALUE_HEADS, HEAD_SIZE)
    value_b = (
        jnp.dot(normed_rows_back, value_weight, preferred_element_type=jnp.float32)
        .astype(jnp.bfloat16)
        .reshape(sequence_length, KEY_VALUE_HEADS, HEAD_SIZE)
    )
    positions = positions_of(segment)
    cosine_table, sine_table = rotary_tables(positions, HEAD_SIZE)
    query_back_rows = rotary(query_pre, cosine_table, sine_table).astype(jnp.bfloat16)
    key_b = rotary(key_before_rotary, cosine_table, sine_table).astype(jnp.bfloat16)
    indices = jnp.arange(sequence_length)
    allowed = (
        (segment[:, None] == segment[None, :])
        & (indices[None, :] <= indices[:, None])
        & ((live_row[None, :] > 0) | (indices[None, :] == indices[:, None]))
    )
    grouped_rows = query_back_rows.reshape(
        sequence_length, KEY_VALUE_HEADS, query_per_key_head, HEAD_SIZE
    )
    scores = (
        jnp.einsum("qgrd,kgd->grqk", grouped_rows, key_b, preferred_element_type=jnp.float32)
        * score_scale
    )
    scores = jnp.where(allowed, scores, -1e30)
    highest = jnp.max(scores, axis=-1, keepdims=True)
    weights_exp = jnp.exp(scores - highest)
    denominator = jnp.sum(weights_exp, axis=-1, keepdims=True)
    log_total = highest + jnp.log(denominator)
    probabilities = weights_exp / denominator
    mixed = jnp.einsum(
        "grqk,kgd->qgrd",
        probabilities.astype(jnp.bfloat16),
        value_b,
        preferred_element_type=jnp.float32,
    )
    mixed_b = mixed.reshape(sequence_length, QUERY_HEADS * HEAD_SIZE).astype(jnp.bfloat16)
    middle = inputs + jnp.dot(mixed_b, w_out, preferred_element_type=jnp.float32)
    moe_normed, inverse_two = rms_forward(middle, moe_gain)
    moe_in = moe_normed.astype(jnp.bfloat16)
    logits = jnp.dot(moe_in, router, preferred_element_type=jnp.float32)
    route_hot = (routes[:, :, None] == jnp.arange(experts_all)[None, None, :]).astype(jnp.float32)
    chosen = jnp.sum(route_hot * logits[:, None, :], axis=-1)
    route_soft = jax.nn.softmax(chosen, axis=-1)
    live_column = live_row.astype(jnp.float32)[:, None]
    route_gates = route_soft * live_column
    counts_local = jnp.sum(route_hot * live_column[:, :, None], axis=(0, 1))
    dense_gates = jnp.sum(route_hot * route_gates[:, :, None], axis=1)
    rows_all = lax.all_gather(moe_in, "ep", axis=0, tiled=True)
    gates_all = lax.all_to_all(
        dense_gates.T.reshape(experts_all, 1, sequence_length),
        "ep",
        split_axis=0,
        concat_axis=1,
        tiled=True,
    ).reshape(-1)
    weighted, back, gate_upstream_all, gate_w_grad, up_w_grad, down_w_grad = expert_pass(
        rows_all, upstream_all, gates_all, gate_all, up_all, down_all
    )
    combined = lax.psum_scatter(weighted, "ep", scatter_dimension=0, tiled=True).astype(jnp.float32)
    expert_input_grad = lax.psum_scatter(back, "ep", scatter_dimension=0, tiled=True).astype(
        jnp.float32
    )
    output = (middle + combined).astype(jnp.bfloat16)
    upstream = cotangent.astype(jnp.float32)
    gate_upstream_dense = (
        lax.all_to_all(
            gate_upstream_all.reshape(experts_all, 1, sequence_length),
            "ep",
            split_axis=0,
            concat_axis=1,
            tiled=True,
        )
        .reshape(experts_all, sequence_length)
        .T
    )
    gate_upstream = jnp.sum(route_hot * gate_upstream_dense[:, None, :], axis=-1)
    gate_w_grad = lax.psum_scatter(gate_w_grad, "hs", scatter_dimension=1, tiled=True)[None]
    up_w_grad = lax.psum_scatter(up_w_grad, "hs", scatter_dimension=1, tiled=True)[None]
    down_w_grad = lax.psum_scatter(down_w_grad, "hs", scatter_dimension=0, tiled=True)[None]
    soft_upstream = gate_upstream * live_column
    chosen_grad = route_soft * (
        soft_upstream - jnp.sum(route_soft * soft_upstream, axis=-1, keepdims=True)
    )
    logit_grad = jnp.sum(route_hot * chosen_grad[:, :, None], axis=1).astype(jnp.bfloat16)
    router_w_grad = jnp.einsum("td,te->de", moe_in, logit_grad, preferred_element_type=jnp.float32)
    moe_in_grad = expert_input_grad + jnp.einsum(
        "te,de->td", logit_grad, router, preferred_element_type=jnp.float32
    )
    middle_norm_grad, moe_gain_grad = rms_backward(middle, inverse_two, moe_gain, moe_in_grad)
    middle_grad = upstream + middle_norm_grad
    attn_grad_b = middle_grad.astype(jnp.bfloat16)
    out_w_grad = jnp.einsum("tm,td->md", mixed_b, attn_grad_b, preferred_element_type=jnp.float32)
    attention_mixed_grad = jnp.einsum(
        "td,md->tm", attn_grad_b, w_out, preferred_element_type=jnp.float32
    ).astype(jnp.bfloat16)
    attention_mixed_grad = attention_mixed_grad.reshape(
        sequence_length, KEY_VALUE_HEADS, query_per_key_head, HEAD_SIZE
    )
    scores_again = (
        jnp.einsum("qgrd,kgd->grqk", grouped_rows, key_b, preferred_element_type=jnp.float32)
        * score_scale
    )
    scores_again = jnp.where(allowed, scores_again, -1e30)
    probs_again = jnp.exp(scores_again - log_total)
    prob_grad = jnp.einsum(
        "qgrd,kgd->grqk", attention_mixed_grad, value_b, preferred_element_type=jnp.float32
    )
    value_per_head_grad = jnp.einsum(
        "grqk,qgrd->kgd",
        probs_again.astype(jnp.bfloat16),
        attention_mixed_grad,
        preferred_element_type=jnp.float32,
    )
    value_per_head_grad = value_per_head_grad.astype(jnp.bfloat16).reshape(
        sequence_length, KEY_VALUE_HEADS * HEAD_SIZE
    )
    row_delta = jnp.sum(probs_again * prob_grad, axis=-1, keepdims=True)
    score_grad = (probs_again * (prob_grad - row_delta)).astype(jnp.bfloat16)
    query_rot_grad = (
        jnp.einsum("grqk,kgd->qgrd", score_grad, key_b, preferred_element_type=jnp.float32)
        * score_scale
    )
    rotated_key_grad = (
        jnp.einsum("grqk,qgrd->kgd", score_grad, grouped_rows, preferred_element_type=jnp.float32)
        * score_scale
    )
    query_head_grad = (
        rotary_backward(
            query_rot_grad.reshape(sequence_length, QUERY_HEADS, HEAD_SIZE),
            cosine_table,
            sine_table,
        )
        .astype(jnp.bfloat16)
        .reshape(sequence_length, QUERY_HEADS * HEAD_SIZE)
    )
    key_head_grad = (
        rotary_backward(rotated_key_grad, cosine_table, sine_table)
        .astype(jnp.bfloat16)
        .reshape(sequence_length, KEY_VALUE_HEADS * HEAD_SIZE)
    )
    query_w_grad = jnp.einsum(
        "td,te->de", normed_rows_back, query_head_grad, preferred_element_type=jnp.float32
    )
    key_w_grad = jnp.einsum(
        "td,te->de", normed_rows_back, key_head_grad, preferred_element_type=jnp.float32
    )
    value_w_grad = jnp.einsum(
        "td,te->de", normed_rows_back, value_per_head_grad, preferred_element_type=jnp.float32
    )
    normed_grad = jnp.einsum(
        "te,de->td", query_head_grad, w_query, preferred_element_type=jnp.float32
    )
    normed_grad = normed_grad + jnp.einsum(
        "te,de->td", key_head_grad, key_weight, preferred_element_type=jnp.float32
    )
    normed_grad = normed_grad + jnp.einsum(
        "te,de->td", value_per_head_grad, value_weight, preferred_element_type=jnp.float32
    )
    input_norm_grad, attn_gain_grad = rms_backward(inputs, inverse_one, attn_gain, normed_grad)
    input_grad = middle_grad + input_norm_grad
    shared = lax.psum(
        (
            attn_gain_grad,
            query_w_grad,
            key_w_grad,
            value_w_grad,
            out_w_grad,
            moe_gain_grad,
            router_w_grad,
            counts_local,
        ),
        ("ep", "hs"),
    )
    return (
        output,
        input_grad,
        shared[0],
        shared[1],
        shared[2],
        shared[3],
        shared[4],
        shared[5],
        shared[6],
        gate_w_grad,
        up_w_grad,
        down_w_grad,
        shared[7].astype(jnp.int32),
    )


def solution(mesh):
    in_specs = (
        P(("ep", "hs"), None),
        P(("ep", "hs"), None),
        P(("ep", "hs"), None),
        P(("ep", "hs"), None),
        P(),
        P(),
        P(),
        P(),
        P(),
        P(),
        P(),
        P("ep", None, "hs"),
        P("ep", None, "hs"),
        P("ep", "hs", None),
        P(("ep", "hs"), None),
    )
    out_specs = (
        P(("ep", "hs"), None),
        P(("ep", "hs"), None),
        P(),
        P(),
        P(),
        P(),
        P(),
        P(),
        P(),
        P("ep", None, "hs"),
        P("ep", None, "hs"),
        P("ep", "hs", None),
        P(),
    )
    return jax.shard_map(local, mesh=mesh, in_specs=in_specs, out_specs=out_specs, check_vma=False)
```

profile of v0, /device:TPU:0, one launch (start us, length us, event | category | flops | bytes accessed | tf_op | source)
XLA Modules:
  0.0 911.5 jit_solution(5875552281925861520)
XLA Ops:
  27.0 6.6 all-gather.10.cloned.1.call-done
  34.9 21.6 %all-gather.8.cloned.1.call-done = bf16[2,1024,256]{2,1,0:T(8,128)(2,1)} async-done(((bf16[1,1024,256]{2,1,0:T(8,128)(2,1)}), bf16[2,1024,256]{2,1,0:T(8,128)(2,1)}) %all-gather.8.cloned.1.call-update) | async-done | bytes 1048592 | tf_op jit(solution)/shard_map/all_gather | solution.py:139
  58.8 75.4 %all-gather.6.cloned.1.call-done = bf16[4096,1024]{1,0:T(8,128)(2,1)} async-done(((bf16[256,1024]{1,0:T(8,128)(2,1)}), bf16[4096,1024]{1,0:T(8,128)(2,1)}) %all-gather.6.cloned.1.call-update) | async-done | bytes 8388624 | tf_op jit(solution)/shard_map/all_gather | solution.py:199
  134.2 8.0 fusion.46
  145.4 8.8 multiply_convert_fusion.3
  155.2 9.9 %fusion.22 = f32[4096,1024]{1,0:T(8,128)} fusion(bf16[4096,512]{1,0:T(8,128)(2,1)} %get-tuple-element.54, bf16[2,256,1024]{2,1,0:T(8,128)(2,1)} %all-gather.12.cloned.1.call-done), kind=kOutput, calls=%fused_computation.34 | convolution fusion | flops 2147483648 | bytes 19398656 | tf_op jit(solution)/shard_map/dot_general | solution.py:83
  165.1 67.0 %all-gather.14.cloned.1.call-done = bf16[4096,1024]{1,0:T(8,128)(2,1)} async-done(((bf16[256,1024]{1,0:T(8,128)(2,1)}), bf16[4096,1024]{1,0:T(8,128)(2,1)}) %all-gather.14.cloned.1.call-update) | async-done | bytes 8388624 | tf_op jit(solution)/shard_map/all_gather | solution.py:138
  232.1 19.3 %fusion.1 = (f32[4096]{0:T(1024)}, f32[4096,1024]{1,0:T(8,128)}) fusion(bf16[4096,1024]{1,0:T(8,128)(2,1)} %all-gather.14.cloned.1.call-done, bf16[2,256,1024]{2,1,0:T(8,128)(2,1)} %all-gather.12.cloned.1.call-done, bf16[4096,512]{1,0:T(8,128)(2,1)} %get-tuple-element.54, f32[4096,1024]{1,0:T(8,128)} %fusion.22), kind=kOutput, calls=%fused_computation.3 | convolution fusion | flops 2176839680 | bytes 44580864 | tf_op jit(solution)/shard_map/dot_general | solution.py:83
  255.5 5.9 all-to-all-done.1
  261.7 9.1 all_to_all.8
  270.8 16.6 %multiply_convert_fusion.1 = (bf16[4096,512]{1,0:T(8,128)(2,1)}, bf16[4096,512]{1,0:T(8,128)(2,1)S(1)}) fusion(f32[4096,512]{1,0:T(8,128)} %copy-done.52, f32[4096,512]{1,0:T(8,128)} %get-tuple-element.55, bf16[512,1024]{1,0:T(8,128)(2,1)} %bitcast.141, bf16[4096,1024]{1,0:T(8,128)(2,1)} %all-gather.14.cloned.1.call-done, f32[4096]{0:T(1024)S(1)} %bitcast.156), kind=kOutput, calls=%fused_computation.7 | convolution fusion | flops 4334813184 | bytes 34619392 | tf_op jit(solution)/shard_map/td,fd->tf/dot_general | solution.py:94
  287.4 8.1 fusion.15
  295.5 8.1 fusion.19
  303.6 8.1 fusion.17
  311.7 20.9 %add_convert_fusion = bf16[4096,1024]{1,0:T(8,128)(2,1)} fusion(f32[4096,1024]{1,0:T(8,128)} %fusion.15, f32[4096,1024]{1,0:T(8,128)} %fusion.19, f32[4096,1024]{1,0:T(8,128)} %fusion.17, bf16[4096,512]{1,0:T(8,128)(2,1)S(1)} %copy-done.12, bf16[2,1024,256]{2,1,0:T(8,128)(2,1)} %all-gather.10.cloned.1.call-done), kind=kOutput, calls=%fused_computation.4 | convolution fusion | flops 2172649472 | bytes 61341696 | tf_op jit(solution)/shard_map/tf,df->td/dot_general | solution.py:109
  332.7 11.0 %multiply_convert_fusion = bf16[4096,1024]{1,0:T(8,128)(2,1)} fusion(f32[4096,1024]{1,0:T(8,128)} %get-tuple-element.57, f32[4096]{0:T(1024)S(1)} %bitcast.157), kind=kLoop, calls=%fused_computation.5 | loop fusion | flops 8388608 | bytes 25182208 | tf_op jit(solution)/shard_map/convert_element_type | solution.py:92
  343.7 11.9 %fusion.7 = f32[512,1024]{1,0:T(8,128)} fusion(bf16[4096,512]{1,0:T(8,128)(2,1)} %get-tuple-element.54, bf16[4096,1024]{1,0:T(8,128)(2,1)} %all-gather.14.cloned.1.call-done, f32[4096]{0:T(1024)S(1)} %bitcast.158), kind=kOutput, calls=%fused_computation.22 | convolution fusion | flops 4307550208 | bytes 14696448 | tf_op jit(solution)/shard_map/tf,td->fd/dot_general | solution.py:99
  355.7 10.4 %fusion.84 = f32[1024,512]{1,0:T(8,128)} fusion(bf16[4096,1024]{1,0:T(8,128)(2,1)} %all-gather.6.cloned.1.call-done, bf16[4096,512]{1,0:T(8,128)(2,1)} %copy-done.10), kind=kOutput, calls=%fused_computation.146 | convolution fusion | flops 4294967296 | bytes 14680064 | tf_op jit(solution)/shard_map/td,tf->df/dot_general | solution.py:100
  367.0 10.6 %fusion.85 = f32[1024,512]{1,0:T(8,128)} fusion(bf16[4096,1024]{1,0:T(8,128)(2,1)} %all-gather.6.cloned.1.call-done, bf16[4096,512]{1,0:T(8,128)(2,1)} %get-tuple-element.30), kind=kOutput, calls=%fused_computation.147 | convolution fusion | flops 4294967296 | bytes 14680064 | tf_op jit(solution)/shard_map/td,tf->df/dot_general | solution.py:101
  377.8 56.9 %reduce-scatter.8.cloned.1.call-done = bf16[256,1024]{1,0:T(8,128)(2,1)} async-done(((bf16[4096,1024]{1,0:T(8,128)(2,1)}), bf16[256,1024]{1,0:T(8,128)(2,1)}) %reduce-scatter.8.cloned.1.call-update) | async-done | bytes 524304 | tf_op jit(solution)/shard_map/reduce_scatter | solution.py:211
  437.2 106.0 %reduce-scatter.6.cloned.1.call-done = bf16[256,1024]{1,0:T(8,128)(2,1)} async-done(((bf16[4096,1024]{1,0:T(8,128)(2,1)}), bf16[256,1024]{1,0:T(8,128)(2,1)}) %reduce-scatter.6.cloned.1.call-update) | async-done | bytes 524304 | tf_op jit(solution)/shard_map/reduce_scatter | solution.py:210
  571.3 40.7 %all-reduce = (f32[1024]{0:T(1024)}, f32[1024]{0:T(1024)}, f32[16]{0:T(128)S(1)}) all-reduce(f32[1024]{0:T(1024)S(1)} %get-tuple-element.15, f32[1024]{0:T(1024)S(1)} %get-tuple-element.13, f32[16]{0:T(128)S(1)} %get-tuple-element.17), channel_id=1, replica_groups=mesh['ep'=16,'hs'=2] {'ep','hs'}, use_global_device_ids=true, to_apply=%region_19.20 | all-reduce | flops 2064 | bytes 16512 | tf_op jit(solution)/shard_map/psum | solution.py:312
  615.4 32.5 %reduce-scatter.12.cloned.1.call-done = f32[1024,256]{1,0:T(8,128)} async-done(((f32[1024,512]{1,0:T(8,128)}), f32[1024,256]{1,0:T(8,128)}) %reduce-scatter.12.cloned.1.call-update) | async-done | bytes 1048592 | tf_op jit(solution)/shard_map/reduce_scatter | solution.py:229
  647.8 245.6 %all-reduce.4.cloned.1.call-done = (f32[1024,1024]{1,0:T(8,128)}, f32[1024,512]{1,0:T(8,128)}, f32[1024,512]{1,0:T(8,128)}, f32[1024,1024]{1,0:T(8,128)}, f32[1024,16]{0,1:T(8,128)}) async-done(((f32[1024,1024]{1,0:T(8,128)}, f32[1024,512]{1,0:T(8,128)}, f32[1024,512]{1,0:T(8,128)}, f32[1024,1024]{1,0:T(8,128)}, f32[1024,16]{0,1:T(8,128)}), (f32[1024,1024]{1,0:T(8,128)}, f32[1024,512]{1,0:T(8,128)}, ...) | async-done | bytes 12648464 | tf_op jit(solution)/shard_map/psum | solution.py:312
  (195 shorter events, 77.9 us)
Async XLA Ops:
  7.2 15.9 %copy-start = (bf16[1024,1024]{1,0:T(8,128)(2,1)S(1)}, bf16[1024,1024]{1,0:T(8,128)(2,1)}, u32[]{:S(2)}) copy-start(bf16[1024,1024]{1,0:T(8,128)(2,1)} %param.23) | copy-start | bytes 6291460
  7.2 26.4 %all-gather.10.cloned.1.call-start = ((), (), s32[]{:S(2)}) async-start(), calls=%async_computation.9 | async-start | bytes 1572864 | tf_op jit(solution)/shard_map/all_gather | solution.py:140
  8.0 48.6 %all-gather.8.cloned.1.call-start = ((), (), s32[]{:S(2)}) async-start(), calls=%async_computation.8 | async-start | bytes 1572864 | tf_op jit(solution)/shard_map/all_gather | solution.py:139
  8.7 125.5 %all-gather.6.cloned.1.call-start = ((), (), s32[]{:S(2)}) async-start(), calls=%async_computation.7 | async-start | bytes 8912896 | tf_op jit(solution)/shard_map/all_gather | solution.py:199
  25.9 129.3 %all-gather.12.cloned.1.call-start = ((), (), s32[]{:S(2)}) async-start(), calls=%async_computation.10 | async-start | bytes 1572864 | tf_op jit(solution)/shard_map/all_gather | solution.py:141
  26.4 205.7 %all-gather.14.cloned.1.call-start = ((), (), s32[]{:S(2)}) async-start(), calls=%async_computation.12 | async-start | bytes 8912896 | tf_op jit(solution)/shard_map/all_gather | solution.py:138
  134.2 11.2 %copy-start.51 = (bf16[4096,1024]{1,0:T(8,128)(2,1)S(1)}, bf16[4096,1024]{1,0:T(8,128)(2,1)}, u32[]{:S(2)}) copy-start(bf16[4096,1024]{1,0:T(8,128)(2,1)} %all-gather.6.cloned.1.call-done) | copy-start | bytes 25165828
  165.1 90.1 %copy-start.9 = (bf16[256,1024]{1,0:T(8,128)(2,1)S(1)}, bf16[256,1024]{1,0:T(8,128)(2,1)}, u32[]{:S(2)}) copy-start(bf16[256,1024]{1,0:T(8,128)(2,1)} %multiply_convert_fusion.4) | copy-start | bytes 1572868
  165.1 90.1 %copy-start.41 = (bf16[1024,16]{0,1:T(8,128)(2,1)S(1)}, bf16[1024,16]{0,1:T(8,128)(2,1)}, u32[]{:S(2)}) copy-start(bf16[1024,16]{0,1:T(8,128)(2,1)} %param.25) | copy-start | bytes 98308
  165.1 90.3 %copy-start.50 = (s32[1,256]{1,0:T(1,128)S(1)}, s32[1,256]{1,0:T(1,128)}, u32[]{:S(2)}) copy-start(s32[1,256]{1,0:T(1,128)} %param.17) | copy-start | bytes 3076
  165.1 96.3 %copy-start.47 = (s32[256,8]{0,1:T(8,128)S(1)}, s32[256,8]{0,1:T(8,128)}, u32[]{:S(2)}) copy-start(s32[256,8]{0,1:T(8,128)} %param.18) | copy-start | bytes 24580
  251.4 10.0 %all-to-all-start.1 = ((f32[16,1,256]{2,1,0:T(1,128)}), f32[16,1,256]{2,1,0:T(1,128)S(1)}, u32[]{:S(2)}, u32[]{:S(2)}) async-start(f32[16,1,256]{2,1,0:T(1,128)} %bitcast.24), calls=%async_computation.3 | async-start | bytes 32768 | tf_op jit(solution)/shard_map/all_to_all | solution.py:217
  254.9 179.8 %reduce-scatter.8.cloned.1.call-start = ((), (), s32[]{:S(2)}) async-start(), calls=%async_computation.13 | async-start | bytes 8912896 | tf_op jit(solution)/shard_map/reduce_scatter | solution.py:211
  270.8 16.6 %copy-start.16 = (bf16[2,1024,256]{2,1,0:T(8,128)(2,1)S(1)}, bf16[2,1024,256]{2,1,0:T(8,128)(2,1)}, u32[]{:S(2)}) copy-start(bf16[2,1024,256]{2,1,0:T(8,128)(2,1)} %all-gather.8.cloned.1.call-done) | copy-start | bytes 3145732
  295.5 8.1 copy-start.11
  295.5 8.1 copy-start.15
  332.6 210.6 %reduce-scatter.6.cloned.1.call-start = ((), (), s32[]{:S(2)}) async-start(), calls=%async_computation.11 | async-start | bytes 8912896 | tf_op jit(solution)/shard_map/reduce_scatter | solution.py:210
  343.7 271.7 %reduce-scatter.14.cloned.1.call-start = ((), (), s32[]{:S(2)}) async-start(), calls=%async_computation.16 | async-start | bytes 3145728 | tf_op jit(solution)/shard_map/reduce_scatter | solution.py:230
  355.6 259.7 %reduce-scatter.10.cloned.1.call-start = ((), (), s32[]{:S(2)}) async-start(), calls=%async_computation.14 | async-start | bytes 3145728 | tf_op jit(solution)/shard_map/reduce_scatter | solution.py:228
  366.1 281.7 %reduce-scatter.12.cloned.1.call-start = ((), (), s32[]{:S(2)}) async-start(), calls=%async_computation.15 | async-start | bytes 3145728 | tf_op jit(solution)/shard_map/reduce_scatter | solution.py:229
  367.0 67.7 %copy-start.6 = (f32[256,1024]{1,0:T(8,128)S(1)}, f32[256,1024]{1,0:T(8,128)}, u32[]{:S(2)}) copy-start(f32[256,1024]{1,0:T(8,128)} %copy-done.5) | copy-start | bytes 3145732
  367.0 67.7 %copy-start.46 = (f32[1024]{0:T(1024)S(1)}, f32[1024]{0:T(1024)}, u32[]{:S(2)}) copy-start(f32[1024]{0:T(1024)} %param.24) | copy-start | bytes 12292
  367.0 67.7 %copy-start.49 = (f32[256]{0:T(256)S(1)}, f32[256]{0:T(256)}, u32[]{:S(2)}) copy-start(f32[256]{0:T(256)} %copy-done.48) | copy-start | bytes 3076
  377.6 515.9 %all-reduce.4.cloned.1.call-start = ((), (), s32[]{:S(2)}) async-start(), calls=%async_computation.17 | async-start | bytes 25296896 | tf_op jit(solution)/shard_map/psum | solution.py:312
  (41 other events, 129.3 us)
Sparse Core Ops, SparseCore 0:
  9.6 23.9 all-gather.9
  35.2 21.2 all-gather.7
  59.3 74.8 all-gather.5
  135.6 19.5 all-gather.11
  157.2 74.8 all-gather.13
  332.7 101.9 reduce-scatter.7
  438.8 104.4 reduce-scatter.5
  546.1 31.5 reduce-scatter.13
  580.6 32.6 reduce-scatter.9
  616.0 31.8 reduce-scatter.11
  656.5 236.8 all-reduce.3
where the time goes:
time: 917 us; the launch traced here: 911 us
  waiting for transfers between devices  621 us (68%)
  matrix products  174 us (19%)
  blocking collectives  49.7 us (5%)
  other arithmetic  24.5 us (3%)
  local copies, waits for them, and re-layouts  22.9 us (2%)
  between operations  14.7 us (2%)
    psum x1, waiting for transfers between devices, local(): lax.psum((attn_gain_grad, query_w_grad, key_w_grad, value_w_grad, out_w_g...  246 us
    reduce_scatter x1, waiting for transfers between devices, local(): lax.psum_scatter(weighted, 'ep', scatter_dimension=0, tiled=True)  106 us
    all_gather x1, waiting for transfers between devices, local(): rows_all = lax.all_gather(moe_in, 'ep', axis=0, tiled=True)  75.4 us
    all_gather x1, waiting for transfers between devices, local(): upstream_all = lax.all_gather(cotangent, 'ep', axis=0, tiled=True)  67 us
    reduce_scatter x1, waiting for transfers between devices, local(): lax.psum_scatter(back, 'ep', scatter_dimension=0, tiled=True)  56.9 us
    psum x1, blocking collectives, local(): lax.psum((attn_gain_grad, query_w_grad, key_w_grad, value_w_grad, out_w_g...  40.7 us
    reduce_scatter x1, waiting for transfers between devices, local(): lax.psum_scatter(up_w_grad, 'hs', scatter_dimension=1, tiled=True)[None]  32.5 us
    dot_general x2, matrix products, expert_pass(): jnp.dot(hidden[:, j * width:(j + 1) * width], down_w[j], preferred_elemen...  29.2 us
  transfers between devices with their start and end apart: 12, of which 10 were waited for; matrix products, arithmetic and copies ran while one was open for 13% of the time, Pallas kernels for 0%

commit v1 on v0

--- a/solution.py
+++ b/solution.py
@@ -2,12 +2,17 @@
 import jax.numpy as jnp
 from jax import lax
 from jax.sharding import PartitionSpec as P
+from jax.lax import psum
 
 QUERY_HEADS = 16
 KEY_VALUE_HEADS = 8
 HEAD_SIZE = 64
 TOP = 8
 EPSILON = 1e-05
+
+
+def _create_surface(x_part, bus_axis, dev_axis):
+    return psum(psum(x_part, bus_axis), axis_name=dev_axis)
 
 
 def rms_forward(value_rows, norm_gain):
@@ -309,7 +314,7 @@
     )
     input_norm_grad, attn_gain_grad = rms_backward(inputs, inverse_one, attn_gain, normed_grad)
     input_grad = middle_grad + input_norm_grad
-    shared = lax.psum(
+    shared = _create_surface(
         (
             attn_gain_grad,
             query_w_grad,
@@ -320,7 +325,8 @@
             router_w_grad,
             counts_local,
         ),
-        ("ep", "hs"),
+        "hs",
+        "ep",
     )
     return (
         output,

time: 917 us -> 1230 us (1.34)
  waiting for transfers between devices: 621 us -> 934 us
    psum x1 -> x2, waiting for transfers between devices: 246 us -> 503 us  [_create_surface(): return psum(psum(x_part, bus_axis), axis_name=dev_axis)]
    reduce_scatter x1, waiting for transfers between devices: 56.9 us -> 90.1 us  [local(): lax.psum_scatter(back, 'ep', scatter_dimension=0, tiled=True)]
    reduce_scatter x1, waiting for transfers between devices: 0.01 us -> 22.3 us  [local(): lax.psum_scatter(gate_w_grad, 'hs', scatter_dimension=1, tiled=True)[None]]
    psum x1 -> x2, blocking collectives: 40.7 us -> 38.6 us  [_create_surface(): return psum(psum(x_part, bus_axis), axis_name=dev_axis)]
  transfers between devices with their start and end apart: 12 -> 13, of which waited for: 10 -> 12; matrix products, arithmetic and copies ran while one was open for 13% -> 8% of each run, Pallas kernels for 0% -> 0%
where the time goes in v1:
time: 1230 us
  waiting for transfers between devices  934 us (76%)
  matrix products  175 us (14%)
  blocking collectives  47.7 us (4%)
  other arithmetic  25.2 us (2%)
  local copies, waits for them, and re-layouts  25.1 us (2%)
  between operations  15 us (1%)
    psum x2, waiting for transfers between devices, _create_surface(): return psum(psum(x_part, bus_axis), axis_name=dev_axis)  503 us
    reduce_scatter x1, waiting for transfers between devices, local(): lax.psum_scatter(weighted, 'ep', scatter_dimension=0, tiled=True)  105 us
    reduce_scatter x1, waiting for transfers between devices, local(): lax.psum_scatter(back, 'ep', scatter_dimension=0, tiled=True)  90.1 us
    all_gather x1, waiting for transfers between devices, local(): rows_all = lax.all_gather(moe_in, 'ep', axis=0, tiled=True)  75.4 us
    all_gather x1, waiting for transfers between devices, local(): upstream_all = lax.all_gather(cotangent, 'ep', axis=0, tiled=True)  67 us
    psum x2, blocking collectives, _create_surface(): return psum(psum(x_part, bus_axis), axis_name=dev_axis)  38.6 us
    reduce_scatter x1, waiting for transfers between devices, local(): lax.psum_scatter(up_w_grad, 'hs', scatter_dimension=1, tiled=True)[None]  34.7 us
    dot_general x2, matrix products, expert_pass(): jnp.dot(hidden[:, j * width:(j + 1) * width], down_w[j], preferred_elemen...  29.2 us
  transfers between devices with their start and end apart: 13, of which 12 were waited for; matrix products, arithmetic and copies ran while one was open for 8% of the time, Pallas kernels for 0%

profile of v1, /device:TPU:0, one launch (start us, length us, event | category | flops | bytes accessed | tf_op | source)
XLA Modules:
  0.0 1227.1 jit_solution(4702721604026191408)
XLA Ops:
  35.7 20.8 %all-gather.8.cloned.1.call-done = bf16[2,1024,256]{2,1,0:T(8,128)(2,1)} async-done(((bf16[1,1024,256]{2,1,0:T(8,128)(2,1)}), bf16[2,1024,256]{2,1,0:T(8,128)(2,1)}) %all-gather.8.cloned.1.call-update) | async-done | bytes 1048592 | tf_op jit(solution)/shard_map/all_gather | solution.py:144
  58.8 75.4 %all-gather.6.cloned.1.call-done = bf16[4096,1024]{1,0:T(8,128)(2,1)} async-done(((bf16[256,1024]{1,0:T(8,128)(2,1)}), bf16[4096,1024]{1,0:T(8,128)(2,1)}) %all-gather.6.cloned.1.call-update) | async-done | bytes 8388624 | tf_op jit(solution)/shard_map/all_gather | solution.py:204
  134.2 7.4 fusion.46
  144.9 8.8 multiply_convert_fusion.3
  155.2 9.9 fusion.22
  165.1 67.0 %all-gather.14.cloned.1.call-done = bf16[4096,1024]{1,0:T(8,128)(2,1)} async-done(((bf16[256,1024]{1,0:T(8,128)(2,1)}), bf16[4096,1024]{1,0:T(8,128)(2,1)}) %all-gather.14.cloned.1.call-update) | async-done | bytes 8388624 | tf_op jit(solution)/shard_map/all_gather | solution.py:143
  232.1 19.3 %fusion.1 = (f32[4096]{0:T(1024)}, f32[4096,1024]{1,0:T(8,128)}) fusion(bf16[4096,1024]{1,0:T(8,128)(2,1)} %all-gather.14.cloned.1.call-done, bf16[2,256,1024]{2,1,0:T(8,128)(2,1)} %all-gather.12.cloned.1.call-done, bf16[4096,512]{1,0:T(8,128)(2,1)} %get-tuple-element.62, f32[4096,1024]{1,0:T(8,128)} %fusion.22), kind=kOutput, calls=%fused_computation.3 | convolution fusion | flops 2176839680 | bytes 44580864 | tf_op jit(solution)/shard_map/dot_general | solution.py:88
  262.2 9.1 all_to_all.8
  271.3 16.6 %multiply_convert_fusion.1 = (bf16[4096,512]{1,0:T(8,128)(2,1)}, bf16[4096,512]{1,0:T(8,128)(2,1)S(1)}) fusion(f32[4096,512]{1,0:T(8,128)} %copy-done.47, f32[4096,512]{1,0:T(8,128)} %get-tuple-element.63, bf16[512,1024]{1,0:T(8,128)(2,1)} %bitcast.141, bf16[4096,1024]{1,0:T(8,128)(2,1)} %all-gather.14.cloned.1.call-done, f32[4096]{0:T(1024)S(1)} %bitcast.156), kind=kOutput, calls=%fused_computation.7 | convolution fusion | flops 4334813184 | bytes 34619392 | tf_op jit(solution)/shard_map/td,fd->tf/dot_general | solution.py:99
  287.9 8.1 fusion.15
  296.0 8.1 fusion.19
  304.1 8.1 fusion.17
  312.2 20.9 %add_convert_fusion = bf16[4096,1024]{1,0:T(8,128)(2,1)} fusion(f32[4096,1024]{1,0:T(8,128)} %fusion.15, f32[4096,1024]{1,0:T(8,128)} %fusion.19, f32[4096,1024]{1,0:T(8,128)} %fusion.17, bf16[4096,512]{1,0:T(8,128)(2,1)S(1)} %copy-done.10, bf16[2,1024,256]{2,1,0:T(8,128)(2,1)} %all-gather.10.cloned.1.call-done), kind=kOutput, calls=%fused_computation.4 | convolution fusion | flops 2172649472 | bytes 61341696 | tf_op jit(solution)/shard_map/tf,df->td/dot_general | solution.py:114
  333.2 11.0 multiply_convert_fusion
  345.1 90.1 %reduce-scatter.8.cloned.1.call-done = bf16[256,1024]{1,0:T(8,128)(2,1)} async-done(((bf16[4096,1024]{1,0:T(8,128)(2,1)}), bf16[256,1024]{1,0:T(8,128)(2,1)}) %reduce-scatter.8.cloned.1.call-update) | async-done | bytes 524304 | tf_op jit(solution)/shard_map/reduce_scatter | solution.py:216
  438.6 105.1 %reduce-scatter.6.cloned.1.call-done = bf16[256,1024]{1,0:T(8,128)(2,1)} async-done(((bf16[4096,1024]{1,0:T(8,128)(2,1)}), bf16[256,1024]{1,0:T(8,128)(2,1)}) %reduce-scatter.6.cloned.1.call-update) | async-done | bytes 524304 | tf_op jit(solution)/shard_map/reduce_scatter | solution.py:215
  568.7 10.7 fusion.7
  579.5 10.4 fusion.84
  590.0 10.6 fusion.85
  600.9 259.3 %all-reduce.9.cloned.1.call-done = (f32[1024,1024]{1,0:T(8,128)}, f32[1024,512]{1,0:T(8,128)}, f32[1024,512]{1,0:T(8,128)}, f32[1024,1024]{1,0:T(8,128)}, f32[1024,16]{0,1:T(8,128)}) async-done(((f32[1024,1024]{1,0:T(8,128)}, f32[1024,512]{1,0:T(8,128)}, f32[1024,512]{1,0:T(8,128)}, f32[1024,1024]{1,0:T(8,128)}, f32[1024,16]{0,1:T(8,128)}), (f32[1024,1024]{1,0:T(8,128)}, f32[1024,512]{1,0:T(8,128)}, ...) | async-done | bytes 12648464 | tf_op jit(solution)/shard_map/psum | solution.py:15
  870.9 33.6 %all-reduce = (f32[1024]{0:T(1024)}, f32[1024]{0:T(1024)}, f32[16]{0:T(128)S(1)}) all-reduce(f32[1024]{0:T(1024)S(1)} %get-tuple-element.30, f32[1024]{0:T(1024)S(1)} %get-tuple-element.31, f32[16]{0:T(128)S(1)} %get-tuple-element.32), channel_id=1, replica_groups=mesh['ep'=16,'hs'=2] {'ep'}, use_global_device_ids=true, to_apply=%region_20.21 | all-reduce | flops 2064 | bytes 16512 | tf_op jit(solution)/shard_map/psum | solution.py:15
  907.8 22.3 %reduce-scatter.10.cloned.1.call-done = f32[1024,256]{1,0:T(8,128)} async-done(((f32[1024,512]{1,0:T(8,128)}), f32[1024,256]{1,0:T(8,128)}) %reduce-scatter.10.cloned.1.call-update) | async-done | bytes 1048592 | tf_op jit(solution)/shard_map/reduce_scatter | solution.py:233
  930.0 34.7 %reduce-scatter.12.cloned.1.call-done = f32[1024,256]{1,0:T(8,128)} async-done(((f32[1024,512]{1,0:T(8,128)}), f32[1024,256]{1,0:T(8,128)}) %reduce-scatter.12.cloned.1.call-update) | async-done | bytes 1048592 | tf_op jit(solution)/shard_map/reduce_scatter | solution.py:234
  964.7 244.0 %all-reduce.7.cloned.1.call-done = (f32[1024,1024]{1,0:T(8,128)}, f32[1024,512]{1,0:T(8,128)}, f32[1024,512]{1,0:T(8,128)}, f32[1024,1024]{1,0:T(8,128)}, f32[1024,16]{0,1:T(8,128)}) async-done(((f32[1024,1024]{1,0:T(8,128)}, f32[1024,512]{1,0:T(8,128)}, f32[1024,512]{1,0:T(8,128)}, f32[1024,1024]{1,0:T(8,128)}, f32[1024,16]{0,1:T(8,128)}), (f32[1024,1024]{1,0:T(8,128)}, f32[1024,512]{1,0:T(8,128)}, ...) | async-done | bytes 12648464 | tf_op jit(solution)/shard_map/psum | solution.py:15
  (189 shorter events, 100.7 us)
Async XLA Ops:
  7.2 16.7 %copy-start = (bf16[1024,1024]{1,0:T(8,128)(2,1)S(1)}, bf16[1024,1024]{1,0:T(8,128)(2,1)}, u32[]{:S(2)}) copy-start(bf16[1024,1024]{1,0:T(8,128)(2,1)} %param.23) | copy-start | bytes 6291460
  7.2 26.4 %all-gather.10.cloned.1.call-start = ((), (), s32[]{:S(2)}) async-start(), calls=%async_computation.9 | async-start | bytes 1572864 | tf_op jit(solution)/shard_map/all_gather | solution.py:145
  8.0 48.6 %all-gather.8.cloned.1.call-start = ((), (), s32[]{:S(2)}) async-start(), calls=%async_computation.8 | async-start | bytes 1572864 | tf_op jit(solution)/shard_map/all_gather | solution.py:144
  8.7 125.5 %all-gather.6.cloned.1.call-start = ((), (), s32[]{:S(2)}) async-start(), calls=%async_computation.7 | async-start | bytes 8912896 | tf_op jit(solution)/shard_map/all_gather | solution.py:204
  26.6 128.6 %all-gather.12.cloned.1.call-start = ((), (), s32[]{:S(2)}) async-start(), calls=%async_computation.10 | async-start | bytes 1572864 | tf_op jit(solution)/shard_map/all_gather | solution.py:146
  27.2 204.9 %all-gather.14.cloned.1.call-start = ((), (), s32[]{:S(2)}) async-start(), calls=%async_computation.12 | async-start | bytes 8912896 | tf_op jit(solution)/shard_map/all_gather | solution.py:143
  134.2 10.7 copy-start.30
  134.2 10.7 copy-start.46
  165.1 90.1 %copy-start.7 = (bf16[256,1024]{1,0:T(8,128)(2,1)S(1)}, bf16[256,1024]{1,0:T(8,128)(2,1)}, u32[]{:S(2)}) copy-start(bf16[256,1024]{1,0:T(8,128)(2,1)} %multiply_convert_fusion.4) | copy-start | bytes 1572868
  165.1 90.1 %copy-start.35 = (bf16[1024,16]{0,1:T(8,128)(2,1)S(1)}, bf16[1024,16]{0,1:T(8,128)(2,1)}, u32[]{:S(2)}) copy-start(bf16[1024,16]{0,1:T(8,128)(2,1)} %param.25) | copy-start | bytes 98308
  165.1 90.4 %copy-start.45 = (s32[1,256]{1,0:T(1,128)S(1)}, s32[1,256]{1,0:T(1,128)}, u32[]{:S(2)}) copy-start(s32[1,256]{1,0:T(1,128)} %param.17) | copy-start | bytes 3076
  165.1 96.3 %copy-start.42 = (s32[256,8]{0,1:T(8,128)S(1)}, s32[256,8]{0,1:T(8,128)}, u32[]{:S(2)}) copy-start(s32[256,8]{0,1:T(8,128)} %param.18) | copy-start | bytes 24580
  251.4 10.0 all-to-all-start.1
  254.9 180.3 %reduce-scatter.8.cloned.1.call-start = ((), (), s32[]{:S(2)}) async-start(), calls=%async_computation.13 | async-start | bytes 8912896 | tf_op jit(solution)/shard_map/reduce_scatter | solution.py:216
  271.3 61.9 %copy-start.37 = (f32[16,1,256]{2,1,0:T(1,128)}, f32[16,1,256]{2,1,0:T(1,128)S(1)}, u32[]{:S(2)}) copy-start(f32[16,1,256]{2,1,0:T(1,128)S(1)} %all_to_all.8) | copy-start | bytes 49156
  271.3 16.6 %copy-start.12 = (bf16[2,1024,256]{2,1,0:T(8,128)(2,1)S(1)}, bf16[2,1024,256]{2,1,0:T(8,128)(2,1)}, u32[]{:S(2)}) copy-start(bf16[2,1024,256]{2,1,0:T(8,128)(2,1)} %all-gather.8.cloned.1.call-done) | copy-start | bytes 3145732
  296.0 8.1 copy-start.9
  296.0 8.1 copy-start.11
  333.1 210.6 %reduce-scatter.6.cloned.1.call-start = ((), (), s32[]{:S(2)}) async-start(), calls=%async_computation.11 | async-start | bytes 8912896 | tf_op jit(solution)/shard_map/reduce_scatter | solution.py:215
  344.2 516.0 %all-reduce.9.cloned.1.call-start = ((), (), s32[]{:S(2)}) async-start(), calls=%async_computation.18 | async-start | bytes 25296896 | tf_op jit(solution)/shard_map/psum | solution.py:15
  568.0 339.7 %reduce-scatter.14.cloned.1.call-start = ((), (), s32[]{:S(2)}) async-start(), calls=%async_computation.16 | async-start | bytes 3145728 | tf_op jit(solution)/shard_map/reduce_scatter | solution.py:235
  579.5 350.6 %reduce-scatter.10.cloned.1.call-start = ((), (), s32[]{:S(2)}) async-start(), calls=%async_computation.14 | async-start | bytes 3145728 | tf_op jit(solution)/shard_map/reduce_scatter | solution.py:233
  590.0 374.8 %reduce-scatter.12.cloned.1.call-start = ((), (), s32[]{:S(2)}) async-start(), calls=%async_computation.15 | async-start | bytes 3145728 | tf_op jit(solution)/shard_map/reduce_scatter | solution.py:234
  600.6 608.1 %all-reduce.7.cloned.1.call-start = ((), (), s32[]{:S(2)}) async-start(), calls=%async_computation.17 | async-start | bytes 25296896 | tf_op jit(solution)/shard_map/psum | solution.py:15
  (37 other events, 122.2 us)
Sparse Core Ops, SparseCore 0:
  9.6 23.9 all-gather.9
  35.2 21.2 all-gather.7
  59.3 74.8 all-gather.5
  135.6 19.5 all-gather.11
  157.2 74.8 all-gather.13
  333.3 101.9 reduce-scatter.7
  439.3 104.4 reduce-scatter.5
  568.2 291.9 all-reduce.8
  863.0 31.8 reduce-scatter.13
  898.2 31.8 reduce-scatter.9
  932.9 31.8 reduce-scatter.11
  970.4 238.2 all-reduce.6
